TPU v7x, 128 devices: a whole 4x4x4 slice. The times are simulated.
128 devices in a mesh: grp: 2 (over core), row: 16 (over y, x), col: 4 (over z).
Axes of the slice: x: 4, y: 4, z: 4, core: 2. Of those that a mesh axis runs over, the one named last changes fastest.
Arguments:
- root_inverse: bfloat16 [12288, 12288], P(('grp', 'row'), 'col'), may hold values from -0.0546875 to 0.0546875
- child_inverse: bfloat16 [2, 8192, 8192], P('grp', 'row', 'col'), may hold values from -0.0625 to 0.0625
- coupling: bfloat16 [2, 1536, 8192], P('grp', 'col', 'row'), may hold values from -0.0625 to 0.0625
- child_weights: bfloat16 [2, 8192], P('grp', 'col'), may hold values from 0.5 to 2
- root_weights: bfloat16 [12288], P('col'), may hold values from 0.5 to 2
- parent_blocks: int32 [2, 12], replicated, may hold values from 0 to 95, as said below
Outputs:
- grad_root: bfloat16 [12288, 12288], P(('grp', 'row'), 'col')
- grad_child: bfloat16 [2, 8192, 8192], P('grp', 'row', 'col')
- grad_coupling: bfloat16 [2, 1536, 8192], P('grp', 'col', 'row')
Inputs may be any that keep to these rules, and one draw needn't show every extreme that they name: `parent_blocks`: within one child the 12 blocks are distinct; child 0 always names block 0 and block 12288 // 128 - 1; the two children may share blocks.
All inputs are finite; a program needn't handle non-finite values.
Results may differ from a plain program's by a relative error of at most 0.0059.
Values may be sent and summed in bfloat16 or wider, within the bound.
A program may use at most 128 MiB of HBM per device.

v0:
```python
import jax
import jax.numpy as jnp
from jax import lax
from jax.sharding import PartitionSpec as P

BW = 128


def local(root_inverse, child_inverse, coupling, child_weights, root_weights, parent_blocks):
    col_index = lax.axis_index("col")
    col_count = lax.axis_size("col")
    root_rows, root_cols = root_inverse.shape
    local_blocks = root_cols // BW
    share_cols = coupling.shape[1]
    width = share_cols * col_count
    block_count = width // BW
    highest = lax.Precision.HIGHEST
    offset = parent_blocks - col_index * local_blocks
    block_ids = jnp.arange(local_blocks, dtype=jnp.int32)
    owners = [
        (offset[child][:, None] == block_ids[None, :]).astype(jnp.float32) for child in range(2)
    ]
    root_blocks = root_inverse.astype(jnp.float32).reshape(root_rows, local_blocks, BW)
    picks = []
    for child in range(2):
        taken = jnp.einsum("rkb,jk->rjb", root_blocks, owners[child], precision=highest)
        picks.append(taken.reshape(root_rows, width))
    picked = jnp.stack(picks, axis=1)
    selected = lax.psum(picked.astype(jnp.bfloat16), "col")
    mine = lax.dynamic_slice_in_dim(selected, col_index * share_cols, share_cols, 2)
    margin_part = jnp.concatenate(
        [
            jnp.dot(selected[:, child, :].T, mine[:, child, :], preferred_element_type=jnp.float32)
            for child in range(2)
        ],
        axis=0,
    )
    margin = lax.psum_scatter(margin_part, ("grp", "row"), scatter_dimension=0, tiled=True).astype(
        jnp.bfloat16
    )
    factor = child_inverse[0]
    links = coupling[0]
    weights = child_weights[0].astype(jnp.float32)
    links_all = lax.all_gather(links, "col", axis=0, tiled=True)
    solved = lax.psum_scatter(
        jnp.dot(links_all, factor, preferred_element_type=jnp.float32),
        "row",
        scatter_dimension=0,
        tiled=True,
    ).astype(jnp.bfloat16)
    solved_all = lax.all_gather(solved, "row", axis=0, tiled=True)
    scaled = (solved.astype(jnp.float32) * weights[None, :]).astype(jnp.bfloat16)
    adjoint_t = lax.psum_scatter(
        jnp.dot(solved_all, scaled.T, preferred_element_type=jnp.float32),
        "col",
        scatter_dimension=0,
        tiled=True,
    ).astype(jnp.bfloat16)
    adjoint_cols = lax.all_gather(adjoint_t, ("grp", "row"), axis=1, tiled=True).reshape(
        share_cols, 2, width
    )
    lifted = jnp.stack(
        [
            jnp.dot(
                selected[:, child, :],
                adjoint_cols[:, child, :].T,
                preferred_element_type=jnp.float32,
            )
            for child in range(2)
        ],
        axis=1,
    ).astype(jnp.bfloat16)
    lifted_all = lax.all_gather(lifted, "col", axis=2, tiled=True).reshape(
        root_rows, 2, block_count, BW
    )
    placed = jnp.zeros((root_rows, local_blocks, BW), jnp.float32)
    for child in range(2):
        spread = lifted_all[:, child].astype(jnp.float32)
        placed = placed + jnp.einsum("rjb,jk->rkb", spread, owners[child], precision=highest)
    placed = placed.reshape(root_rows, root_cols)
    root_scale = root_weights.astype(jnp.float32)[None, :]
    grad_root = (2.0 * root_inverse.astype(jnp.float32) * root_scale + 2.0 * placed).astype(
        jnp.bfloat16
    )
    margin_row = lax.all_gather(margin, "col", axis=1, tiled=True)
    pulled = (
        2.0 * jnp.dot(margin_row, solved_all, preferred_element_type=jnp.float32) * weights[None, :]
    ).astype(jnp.bfloat16)
    pulled_all = lax.all_gather(pulled, "row", axis=0, tiled=True)
    grad_links = lax.psum_scatter(
        jnp.dot(pulled_all, factor.T, preferred_element_type=jnp.float32),
        "col",
        scatter_dimension=0,
        tiled=True,
    ).astype(jnp.bfloat16)
    grad_factor = jnp.dot(links_all.T, pulled_all, preferred_element_type=jnp.float32)
    grad_factor = (grad_factor + 2.0 * factor.astype(jnp.float32) * weights[None, :]).astype(
        jnp.bfloat16
    )
    return (grad_root, grad_factor[None], grad_links[None])


def solution(mesh):
    return jax.shard_map(
        local,
        mesh=mesh,
        in_specs=(
            P(("grp", "row"), "col"),
            P("grp", "row", "col"),
            P("grp", "col", "row"),
            P("grp", "col"),
            P("col"),
            P(),
        ),
        out_specs=(P(("grp", "row"), "col"), P("grp", "row", "col"), P("grp", "col", "row")),
        check_vma=False,
    )
```

profile of v0, /device:TPU:1, one launch (start us, length us, event | category | flops | bytes accessed | tf_op | source)
XLA Modules:
  0.0 578.5 jit_solution(17137444513439801942)
XLA Ops:
  7.2 0.0 all-gather.15.cloned.1.call-start
  7.2 0.7 all-gather.15.cloned.1.call-update
  7.9 0.0 reduce-scatter.5.cloned.1.call-start
  7.9 31.4 %all-gather.15.cloned.1.call-done = bf16[1,1536,512]{2,1,0:T(8,128)(2,1)} async-done(((bf16[1,384,512]{2,1,0:T(8,128)(2,1)}), bf16[1,1536,512]{2,1,0:T(8,128)(2,1)}) %all-gather.15.cloned.1.call-update) | async-done | bytes 1572880 | tf_op jit(solution)/shard_map/all_gather | solution.py:44
  39.4 10.0 %fusion.6 = f32[1536,2048]{1,0:T(8,128)} fusion(bf16[1,512,2048]{2,1,0:T(8,128)(2,1)} %param.7, bf16[1,1536,512]{2,1,0:T(8,128)(2,1)} %all-gather.15.cloned.1.call-done), kind=kOutput, calls=%fused_computation.12 | convolution fusion | flops 3221225472 | bytes 16252928 | tf_op jit(solution)/shard_map/dot_general | solution.py:46
  49.4 0.0 reduce-scatter.5.cloned.1.call-update
  49.4 0.0 all-gather.7.cloned.1.call-start
  49.5 94.5 %reduce-scatter.5.cloned.1.call-done = f32[96,2048]{1,0:T(8,128)} async-done(((f32[1536,2048]{1,0:T(8,128)}), f32[96,2048]{1,0:T(8,128)}) %reduce-scatter.5.cloned.1.call-update) | async-done | bytes 786448 | tf_op jit(solution)/shard_map/reduce_scatter | solution.py:45
  144.0 1.9 convert_element_type.47
  145.9 0.0 all-gather.7.cloned.1.call-update
  145.9 0.0 all-reduce.2.cloned.1.call-start
  146.0 2.2 copy.20
  148.3 0.6 copy-done.9
  148.8 1.8 fusion.13
  150.6 2.1 copy.11
  152.8 1.8 fusion.14
  154.6 2.2 copy.12
  156.7 1.7 pad_maximum_fusion.1
  158.4 0.0 all-reduce.2.cloned.1.call-update
  158.4 0.0 reduce-scatter.7.cloned.1.call-start
  158.5 0.6 copy-done.7
  159.1 48.1 %all-gather.7.cloned.1.call-done = bf16[1536,2048]{1,0:T(8,128)(2,1)} async-done(((bf16[96,2048]{1,0:T(8,128)(2,1)}), bf16[1536,2048]{1,0:T(8,128)(2,1)}) %all-gather.7.cloned.1.call-update) | async-done | bytes 6291472 | tf_op jit(solution)/shard_map/all_gather | solution.py:51
  207.2 5.7 fusion.19
  212.9 0.0 reduce-scatter.7.cloned.1.call-update
  212.9 0.0 reduce-scatter.9.cloned.1.call-start
  213.0 60.0 %all-reduce.2.cloned.1.call-done = bf16[384,2,1536]{0,2,1:T(8,128)(2,1)} async-done(((bf16[384,2,1536]{0,2,1:T(8,128)(2,1)}), bf16[384,2,1536]{0,2,1:T(8,128)(2,1)}) %all-reduce.2.cloned.1.call-update) | async-done | bytes 2359312 | tf_op jit(solution)/shard_map/psum | solution.py:29
  273.0 2.4 fusion.17
  275.4 0.9 fusion.18
  276.3 2.5 pad_maximum_fusion
  278.8 0.0 reduce-scatter.9.cloned.1.call-update
  278.8 0.0 all-gather.9.cloned.1.call-start
  278.9 16.9 %reduce-scatter.7.cloned.1.call-done = f32[384,96]{0,1:T(8,128)} async-done(((f32[1536,96]{0,1:T(8,128)}), f32[384,96]{0,1:T(8,128)}) %reduce-scatter.7.cloned.1.call-update) | async-done | bytes 147472 | tf_op jit(solution)/shard_map/reduce_scatter | solution.py:53
  295.8 1.6 convert_element_type.50
  297.4 0.0 all-gather.9.cloned.1.call-update
  297.4 0.0 all-gather.13.cloned.1.call-start
  297.5 85.5 %reduce-scatter.9.cloned.1.call-done = f32[96,384]{1,0:T(8,128)} async-done(((f32[3072,384]{1,0:T(8,128)}), f32[96,384]{1,0:T(8,128)}) %reduce-scatter.9.cloned.1.call-update) | async-done | bytes 147472 | tf_op jit(solution)/shard_map/reduce_scatter | solution.py:38
  383.0 0.9 convert_element_type.52
  383.9 10.0 %all_gather.22 = bf16[96,1536]{1,0:T(8,128)(2,1)S(1)} all-gather(bf16[96,384]{1,0:T(8,128)(2,1)S(1)} %convert_element_type.52), channel_id=1, replica_groups=mesh['grp'=2,'row'=16,'col'=4] {'col'}, dimensions={1}, use_global_device_ids=true | all-gather | bytes 368640 | tf_op jit(solution)/shard_map/all_gather | solution.py:85
  394.0 4.7 fusion.3
  398.7 0.0 all-gather.13.cloned.1.call-update
  398.7 0.2 all-gather.11.cloned.1.call-start
  399.0 32.1 %all-gather.9.cloned.1.call-done = bf16[384,3072]{0,1:T(8,128)(2,1)} async-done(((bf16[384,96]{0,1:T(8,128)(2,1)}), bf16[384,3072]{0,1:T(8,128)(2,1)}) %all-gather.9.cloned.1.call-update) | async-done | bytes 2359312 | tf_op jit(solution)/shard_map/all_gather | solution.py:59
  431.0 2.2 fusion.15
  433.3 0.8 fusion.16
  434.1 0.9 pad_maximum_fusion.2
  435.0 0.0 reduce-scatter.11.cloned.1.call-start
  435.0 58.7 %all-gather.13.cloned.1.call-done = bf16[1536,2048]{1,0:T(8,128)(2,1)} async-done(((bf16[96,2048]{1,0:T(8,128)(2,1)}), bf16[1536,2048]{1,0:T(8,128)(2,1)}) %all-gather.13.cloned.1.call-update) | async-done | bytes 6291472 | tf_op jit(solution)/shard_map/all_gather | solution.py:89
  493.8 8.6 %fusion.4 = f32[1536,512]{1,0:T(8,128)} fusion(bf16[1536,2048]{1,0:T(8,128)(2,1)} %all-gather.13.cloned.1.call-done, bf16[1,512,2048]{2,1,0:T(8,128)(2,1)} %param.7), kind=kOutput, calls=%fused_computation.10 | convolution fusion | flops 3221225472 | bytes 11534336 | tf_op jit(solution)/shard_map/dot_general | solution.py:91
  502.4 0.0 reduce-scatter.11.cloned.1.call-update
  502.4 1.6 copy-done.3
  504.0 2.5 copy.13
  506.5 22.5 %all-gather.11.cloned.1.call-done = bf16[384,2,1536]{2,0,1:T(8,128)(2,1)} async-done(((bf16[384,2,384]{2,0,1:T(8,128)(2,1)}), bf16[384,2,1536]{2,0,1:T(8,128)(2,1)}) %all-gather.11.cloned.1.call-update) | async-done | bytes 2359312 | tf_op jit(solution)/shard_map/all_gather | solution.py:73
  528.9 3.0 copy.14
  532.0 1.3 fusion.33
  533.3 1.4 copy.18
  534.7 2.3 copy.19
  537.0 0.9 fusion.9
  537.9 0.9 add_multiply_fusion
  538.9 1.1 copy-done
  540.0 2.9 fusion
  542.9 3.7 fusion.2
  546.6 2.4 copy.17
  549.0 20.8 %reduce-scatter.11.cloned.1.call-done = f32[384,512]{1,0:T(8,128)} async-done(((f32[1536,512]{1,0:T(8,128)}), f32[384,512]{1,0:T(8,128)}) %reduce-scatter.11.cloned.1.call-update) | async-done | bytes 786448 | tf_op jit(solution)/shard_map/reduce_scatter | solution.py:90
  569.7 1.9 convert_bitcast_fusion
  (35 shorter events, 0.1 us)
Async XLA Ops:
  7.2 32.2 %all-gather.15.cloned.1.call-start = ((), (), s32[]{:S(2)}) async-start(), calls=%async_computation.13 | async-start | bytes 1966080 | tf_op jit(solution)/shard_map/all_gather | solution.py:44
  7.9 136.1 %reduce-scatter.5.cloned.1.call-start = ((), (), s32[]{:S(2)}) async-start(), calls=%async_computation.5 | async-start | bytes 13369344 | tf_op jit(solution)/shard_map/reduce_scatter | solution.py:45
  49.4 157.8 %all-gather.7.cloned.1.call-start = ((), (), s32[]{:S(2)}) async-start(), calls=%async_computation.6 | async-start | bytes 6684672 | tf_op jit(solution)/shard_map/all_gather | solution.py:51
  145.9 127.1 %all-reduce.2.cloned.1.call-start = ((), (), s32[]{:S(2)}) async-start(), calls=%async_computation.4 | async-start | bytes 4718592 | tf_op jit(solution)/shard_map/psum | solution.py:29
  146.0 2.3 copy-start.11
  148.3 0.6 copy-start.9
  158.4 0.7 copy-start.7
  158.4 48.8 %copy-start.1 = (bf16[96,2048]{1,0:T(8,128)(2,1)S(1)}, bf16[96,2048]{1,0:T(8,128)(2,1)}, u32[]{:S(2)}) copy-start(bf16[96,2048]{1,0:T(8,128)(2,1)} %convert_element_type.47) | copy-start | bytes 1179652
  158.4 137.4 %reduce-scatter.7.cloned.1.call-start = ((), (), s32[]{:S(2)}) async-start(), calls=%async_computation.7 | async-start | bytes 737280 | tf_op jit(solution)/shard_map/reduce_scatter | solution.py:53
  212.9 170.1 %reduce-scatter.9.cloned.1.call-start = ((), (), s32[]{:S(2)}) async-start(), calls=%async_computation.10 | async-start | bytes 4866048 | tf_op jit(solution)/shard_map/reduce_scatter | solution.py:38
  273.0 2.4 copy-start.2
  278.8 152.2 %all-gather.9.cloned.1.call-start = ((), (), s32[]{:S(2)}) async-start(), calls=%async_computation.8 | async-start | bytes 2433024 | tf_op jit(solution)/shard_map/all_gather | solution.py:59
  297.4 196.4 %all-gather.13.cloned.1.call-start = ((), (), s32[]{:S(2)}) async-start(), calls=%async_computation.11 | async-start | bytes 6684672 | tf_op jit(solution)/shard_map/all_gather | solution.py:89
  297.5 101.2 %copy-start.5 = (f32[2048]{0:T(1024)}, f32[2048]{0:T(1024)S(1)}, u32[]{:S(2)}) copy-start(f32[2048]{0:T(1024)S(1)} %broadcast_multiply_fusion) | copy-start | bytes 24580
  398.7 130.2 %all-gather.11.cloned.1.call-start = ((), (), s32[]{:S(2)}) async-start(), calls=%async_computation.9 | async-start | bytes 2949120 | tf_op jit(solution)/shard_map/all_gather | solution.py:73
  431.0 2.2 copy-start.12
  435.0 134.8 %reduce-scatter.11.cloned.1.call-start = ((), (), s32[]{:S(2)}) async-start(), calls=%async_computation.12 | async-start | bytes 3932160 | tf_op jit(solution)/shard_map/reduce_scatter | solution.py:90
  502.4 1.6 copy-start.3
  504.0 2.5 copy-start.8
  534.7 2.3 copy-start.10
  537.0 5.8 %slice-start = ((s8[6291456]{0:T(1024)(128)(4,1)}), s8[4194304]{0:T(1024)(128)(4,1)S(1)}, s32[]{:S(2)}) async-start(s8[6291456]{0:T(1024)(128)(4,1)} %bitcast.102), calls=%async_computation.14 | async-start | bytes 8388608
  537.9 2.0 copy-start
  537.9 4.9 slice-start.1
  539.9 2.9 copy-start.4
  539.9 2.9 copy-start.6
  540.0 2.9 copy-start.13
Sparse Core Ops, SparseCore 0:
  9.6 29.7 all-gather.14
  49.5 94.3 reduce-scatter.4
  146.7 60.5 all-gather.6
  210.0 62.8 all-reduce.1
  275.8 19.9 reduce-scatter.6
  299.4 83.5 reduce-scatter.8
  385.8 45.1 all-gather.8
  433.7 59.9 all-gather.12
  496.0 32.8 all-gather.10
  531.2 38.4 reduce-scatter.10
where the time goes:
time: 579 us
  waiting for transfers between devices  471 us (81%)
  matrix products  44.4 us (8%)
  local copies, waits for them, and re-layouts  23.3 us (4%)
  between operations  14.4 us (2%)
  other arithmetic  14.3 us (2%)
  blocking collectives  10 us (2%)
    reduce_scatter x1, waiting for transfers between devices, local(): lax.psum_scatter(jnp.dot(links_all, factor, preferred_element_type=jnp.fl...  94.5 us
    reduce_scatter x1, waiting for transfers between devices, local(): lax.psum_scatter(margin_part, ('grp', 'row'), scatter_dimension=0, tiled=...  85.5 us
    psum x1, waiting for transfers between devices, local(): selected = lax.psum(picked.astype(jnp.bfloat16), 'col')  60 us
    all_gather x1, waiting for transfers between devices, local(): pulled_all = lax.all_gather(pulled, 'row', axis=0, tiled=True)  58.7 us
    all_gather x1, waiting for transfers between devices, local(): solved_all = lax.all_gather(solved, 'row', axis=0, tiled=True)  48.1 us
    all_gather x1, waiting for transfers between devices, local(): lax.all_gather(adjoint_t, ('grp', 'row'), axis=1, tiled=True)  32.1 us
    all_gather x1, waiting for transfers between devices, local(): links_all = lax.all_gather(links, 'col', axis=0, tiled=True)  31.4 us
    all_gather x1, waiting for transfers between devices, local(): lax.all_gather(lifted, 'col', axis=2, tiled=True)  22.5 us
  transfers between devices with their start and end apart: 10, of which 10 were waited for; matrix products, arithmetic and copies ran while one was open for 11% of the time, Pallas kernels for 0%

commit v1 on v0

--- a/solution.py
+++ b/solution.py
@@ -26,7 +26,7 @@
         taken = jnp.einsum("rkb,jk->rjb", root_blocks, owners[child], precision=highest)
         picks.append(taken.reshape(root_rows, width))
     picked = jnp.stack(picks, axis=1)
-    selected = lax.psum(picked.astype(jnp.bfloat16), "col")
+    selected = jnp.sum(lax.all_gather(picked.astype(jnp.bfloat16), "col"), axis=0)
     mine = lax.dynamic_slice_in_dim(selected, col_index * share_cols, share_cols, 2)
     margin_part = jnp.concatenate(
         [

time: 579 us -> 609 us (1.052)
  waiting for transfers between devices: 471 us -> 493 us
    all_gather x0 -> x1, waiting for transfers between devices: none -> 87.9 us  [local(): lax.all_gather(picked.astype(jnp.bfloat16), 'col')]
    psum x1 -> x0, waiting for transfers between devices: 60 us -> none  [local(): selected = lax.psum(picked.astype(jnp.bfloat16), 'col')]
    unnamed x37 -> x35, local copies, waits for them, and re-layouts: 14.7 us -> 14.7 us
  transfers between devices with their start and end apart: 10 -> 10, of which waited for: 10 -> 10; matrix products, arithmetic and copies ran while one was open for 11% -> 12% of each run, Pallas kernels for 0% -> 0%
where the time goes in v1:
time: 609 us; the launch traced here: 608 us
  waiting for transfers between devices  493 us (81%)
  matrix products  42.9 us (7%)
  local copies, waits for them, and re-layouts  26.5 us (4%)
  other arithmetic  20 us (3%)
  between operations  14.4 us (2%)
  blocking collectives  10 us (2%)
    reduce_scatter x1, waiting for transfers between devices, local(): lax.psum_scatter(jnp.dot(links_all, factor, preferred_element_type=jnp.fl...  94.5 us
    all_gather x1, waiting for transfers between devices, local(): lax.all_gather(picked.astype(jnp.bfloat16), 'col')  87.9 us
    reduce_scatter x1, waiting for transfers between devices, local(): lax.psum_scatter(margin_part, ('grp', 'row'), scatter_dimension=0, tiled=...  85.6 us
    all_gather x1, waiting for transfers between devices, local(): pulled_all = lax.all_gather(pulled, 'row', axis=0, tiled=True)  58.6 us
    all_gather x1, waiting for transfers between devices, local(): solved_all = lax.all_gather(solved, 'row', axis=0, tiled=True)  45.1 us
    all_gather x1, waiting for transfers between devices, local(): lax.all_gather(adjoint_t, ('grp', 'row'), axis=1, tiled=True)  32.2 us
    all_gather x1, waiting for transfers between devices, local(): links_all = lax.all_gather(links, 'col', axis=0, tiled=True)  31.4 us
    all_gather x1, waiting for transfers between devices, local(): lax.all_gather(lifted, 'col', axis=2, tiled=True)  22.5 us
  transfers between devices with their start and end apart: 10, of which 10 were waited for; matrix products, arithmetic and copies ran while one was open for 12% of the time, Pallas kernels for 0%

profile of v1, /device:TPU:1, one launch (start us, length us, event | category | flops | bytes accessed | tf_op | source)
XLA Modules:
  0.0 607.9 jit_solution(6036884127559897906)
XLA Ops:
  7.2 0.0 all-gather.18.cloned.1.call-start
  7.2 0.7 all-gather.18.cloned.1.call-update
  7.9 0.0 reduce-scatter.5.cloned.1.call-start
  7.9 31.4 %all-gather.18.cloned.1.call-done = bf16[1,1536,512]{2,1,0:T(8,128)(2,1)} async-done(((bf16[1,384,512]{2,1,0:T(8,128)(2,1)}), bf16[1,1536,512]{2,1,0:T(8,128)(2,1)}) %all-gather.18.cloned.1.call-update) | async-done | bytes 1572880 | tf_op jit(solution)/shard_map/all_gather | solution.py:44
  39.4 10.0 %fusion.6 = f32[1536,2048]{1,0:T(8,128)} fusion(bf16[1,512,2048]{2,1,0:T(8,128)(2,1)} %param.7, bf16[1,1536,512]{2,1,0:T(8,128)(2,1)} %all-gather.18.cloned.1.call-done), kind=kOutput, calls=%fused_computation.12 | convolution fusion | flops 3221225472 | bytes 16252928 | tf_op jit(solution)/shard_map/dot_general | solution.py:46
  49.4 0.0 reduce-scatter.5.cloned.1.call-update
  49.4 0.0 all-gather.10.cloned.1.call-start
  49.5 94.5 %reduce-scatter.5.cloned.1.call-done = f32[96,2048]{1,0:T(8,128)} async-done(((f32[1536,2048]{1,0:T(8,128)}), f32[96,2048]{1,0:T(8,128)}) %reduce-scatter.5.cloned.1.call-update) | async-done | bytes 786448 | tf_op jit(solution)/shard_map/reduce_scatter | solution.py:45
  144.0 1.9 convert_element_type.56
  145.9 0.0 all-gather.10.cloned.1.call-update
  145.9 0.0 all-gather.8.cloned.1.call-start
  146.0 2.2 copy.39
  148.3 0.6 copy-done.8
  148.8 1.8 fusion.13
  150.6 2.1 copy.18
  152.8 1.8 fusion.14
  154.6 2.7 copy.19
  157.3 1.5 pad_maximum_fusion.1
  158.9 2.6 copy.20
  161.5 0.0 all-gather.8.cloned.1.call-update
  161.5 0.0 reduce-scatter.7.cloned.1.call-start
  161.5 0.6 copy-done.6
  162.2 45.1 %all-gather.10.cloned.1.call-done = bf16[1536,2048]{1,0:T(8,128)(2,1)} async-done(((bf16[96,2048]{1,0:T(8,128)(2,1)}), bf16[1536,2048]{1,0:T(8,128)(2,1)}) %all-gather.10.cloned.1.call-update) | async-done | bytes 6291472 | tf_op jit(solution)/shard_map/all_gather | solution.py:51
  207.2 5.7 fusion.19
  212.9 0.2 reduce-scatter.9.cloned.1.call-start
  213.2 87.9 %all-gather.8.cloned.1.call-done = bf16[4,384,2,1536]{3,1,2,0:T(8,128)(2,1)} async-done(((bf16[1,384,2,1536]{3,1,2,0:T(8,128)(2,1)}), bf16[4,384,2,1536]{3,1,2,0:T(8,128)(2,1)}) %all-gather.8.cloned.1.call-update) | async-done | bytes 9437200 | tf_op jit(solution)/shard_map/all_gather | solution.py:29
  301.1 5.9 reduce_sum.12
  307.0 0.9 fusion.17
  308.0 0.9 fusion.18
  308.9 2.4 pad_maximum_fusion
  311.4 0.0 all-gather.12.cloned.1.call-start
  311.4 13.8 %reduce-scatter.7.cloned.1.call-done = f32[384,96]{0,1:T(8,128)} async-done(((f32[1536,96]{0,1:T(8,128)}), f32[384,96]{0,1:T(8,128)}) %reduce-scatter.7.cloned.1.call-update) | async-done | bytes 147472 | tf_op jit(solution)/shard_map/reduce_scatter | solution.py:53
  325.2 1.6 convert_element_type.59
  326.8 0.0 all-gather.16.cloned.1.call-start
  326.9 85.6 %reduce-scatter.9.cloned.1.call-done = f32[96,384]{1,0:T(8,128)} async-done(((f32[3072,384]{1,0:T(8,128)}), f32[96,384]{1,0:T(8,128)}) %reduce-scatter.9.cloned.1.call-update) | async-done | bytes 147472 | tf_op jit(solution)/shard_map/reduce_scatter | solution.py:38
  412.4 0.9 convert_element_type.61
  413.3 10.0 %all_gather.27 = bf16[96,1536]{1,0:T(8,128)(2,1)S(1)} all-gather(bf16[96,384]{1,0:T(8,128)(2,1)S(1)} %convert_element_type.61), channel_id=1, replica_groups=mesh['grp'=2,'row'=16,'col'=4] {'col'}, dimensions={1}, use_global_device_ids=true | all-gather | bytes 368640 | tf_op jit(solution)/shard_map/all_gather | solution.py:85
  423.4 4.7 fusion.3
  428.1 0.0 all-gather.16.cloned.1.call-update
  428.1 0.0 all-gather.14.cloned.1.call-start
  428.2 32.2 %all-gather.12.cloned.1.call-done = bf16[384,3072]{0,1:T(8,128)(2,1)} async-done(((bf16[384,96]{0,1:T(8,128)(2,1)}), bf16[384,3072]{0,1:T(8,128)(2,1)}) %all-gather.12.cloned.1.call-update) | async-done | bytes 2359312 | tf_op jit(solution)/shard_map/all_gather | solution.py:59
  460.4 2.2 fusion.15
  462.6 0.8 fusion.16
  463.4 0.9 pad_maximum_fusion.2
  464.3 0.0 all-gather.14.cloned.1.call-update
  464.3 0.3 reduce-scatter.11.cloned.1.call-start
  464.6 58.6 %all-gather.16.cloned.1.call-done = bf16[1536,2048]{1,0:T(8,128)(2,1)} async-done(((bf16[96,2048]{1,0:T(8,128)(2,1)}), bf16[1536,2048]{1,0:T(8,128)(2,1)}) %all-gather.16.cloned.1.call-update) | async-done | bytes 6291472 | tf_op jit(solution)/shard_map/all_gather | solution.py:89
  523.2 8.6 %fusion.4 = f32[1536,512]{1,0:T(8,128)} fusion(bf16[1536,2048]{1,0:T(8,128)(2,1)} %all-gather.16.cloned.1.call-done, bf16[1,512,2048]{2,1,0:T(8,128)(2,1)} %param.7), kind=kOutput, calls=%fused_computation.10 | convolution fusion | flops 3221225472 | bytes 11534336 | tf_op jit(solution)/shard_map/dot_general | solution.py:91
  531.8 0.0 reduce-scatter.11.cloned.1.call-update
  531.8 1.6 copy-done.2
  533.4 2.5 copy.23
  535.9 22.5 %all-gather.14.cloned.1.call-done = bf16[384,2,1536]{2,0,1:T(8,128)(2,1)} async-done(((bf16[384,2,384]{2,0,1:T(8,128)(2,1)}), bf16[384,2,1536]{2,0,1:T(8,128)(2,1)}) %all-gather.14.cloned.1.call-update) | async-done | bytes 2359312 | tf_op jit(solution)/shard_map/all_gather | solution.py:73
  558.3 3.0 copy.25
  561.4 1.3 fusion.33
  562.7 1.4 copy.34
  564.1 2.3 copy.35
  566.4 0.9 fusion.9
  567.3 0.9 add_multiply_fusion
  568.3 1.1 copy-done
  569.4 2.9 fusion
  572.3 3.7 fusion.2
  576.0 2.4 copy.30
  578.4 20.8 %reduce-scatter.11.cloned.1.call-done = f32[384,512]{1,0:T(8,128)} async-done(((f32[1536,512]{1,0:T(8,128)}), f32[384,512]{1,0:T(8,128)}) %reduce-scatter.11.cloned.1.call-update) | async-done | bytes 786448 | tf_op jit(solution)/shard_map/reduce_scatter | solution.py:90
  599.1 1.9 convert_bitcast_fusion
  (35 shorter events, 0.1 us)
Async XLA Ops:
  7.2 32.2 %all-gather.18.cloned.1.call-start = ((), (), s32[]{:S(2)}) async-start(), calls=%async_computation.13 | async-start | bytes 1966080 | tf_op jit(solution)/shard_map/all_gather | solution.py:44
  7.9 136.1 %reduce-scatter.5.cloned.1.call-start = ((), (), s32[]{:S(2)}) async-start(), calls=%async_computation.5 | async-start | bytes 13369344 | tf_op jit(solution)/shard_map/reduce_scatter | solution.py:45
  49.4 157.8 %all-gather.10.cloned.1.call-start = ((), (), s32[]{:S(2)}) async-start(), calls=%async_computation.6 | async-start | bytes 6684672 | tf_op jit(solution)/shard_map/all_gather | solution.py:51
  145.9 155.2 %all-gather.8.cloned.1.call-start = ((), (), s32[]{:S(2)}) async-start(), calls=%async_computation.4 | async-start | bytes 11796480 | tf_op jit(solution)/shard_map/all_gather | solution.py:29
  146.0 2.3 copy-start.10
  148.3 0.6 copy-start.8
  161.5 0.7 copy-start.6
  161.5 45.8 %copy-start.1 = (bf16[96,2048]{1,0:T(8,128)(2,1)S(1)}, bf16[96,2048]{1,0:T(8,128)(2,1)}, u32[]{:S(2)}) copy-start(bf16[96,2048]{1,0:T(8,128)(2,1)} %convert_element_type.56) | copy-start | bytes 1179652
  161.5 163.7 %reduce-scatter.7.cloned.1.call-start = ((), (), s32[]{:S(2)}) async-start(), calls=%async_computation.7 | async-start | bytes 737280 | tf_op jit(solution)/shard_map/reduce_scatter | solution.py:53
  212.9 199.5 %reduce-scatter.9.cloned.1.call-start = ((), (), s32[]{:S(2)}) async-start(), calls=%async_computation.10 | async-start | bytes 4866048 | tf_op jit(solution)/shard_map/reduce_scatter | solution.py:38
  311.4 149.0 %all-gather.12.cloned.1.call-start = ((), (), s32[]{:S(2)}) async-start(), calls=%async_computation.8 | async-start | bytes 2433024 | tf_op jit(solution)/shard_map/all_gather | solution.py:59
  326.8 196.4 %all-gather.16.cloned.1.call-start = ((), (), s32[]{:S(2)}) async-start(), calls=%async_computation.11 | async-start | bytes 6684672 | tf_op jit(solution)/shard_map/all_gather | solution.py:89
  326.8 101.3 %copy-start.4 = (f32[2048]{0:T(1024)}, f32[2048]{0:T(1024)S(1)}, u32[]{:S(2)}) copy-start(f32[2048]{0:T(1024)S(1)} %broadcast_multiply_fusion) | copy-start | bytes 24580
  428.1 130.2 %all-gather.14.cloned.1.call-start = ((), (), s32[]{:S(2)}) async-start(), calls=%async_computation.9 | async-start | bytes 2949120 | tf_op jit(solution)/shard_map/all_gather | solution.py:73
  460.4 2.2 copy-start.11
  464.3 134.8 %reduce-scatter.11.cloned.1.call-start = ((), (), s32[]{:S(2)}) async-start(), calls=%async_computation.12 | async-start | bytes 3932160 | tf_op jit(solution)/shard_map/reduce_scatter | solution.py:90
  531.8 1.6 copy-start.2
  533.4 2.5 copy-start.7
  564.1 2.3 copy-start.9
  566.4 5.8 slice-start
  567.3 2.0 copy-start
  567.3 4.9 slice-start.1
  569.3 2.9 copy-start.3
  569.3 2.9 copy-start.5
  569.3 2.9 copy-start.12
Sparse Core Ops, SparseCore 0:
  9.6 29.7 all-gather.17
  49.5 94.3 reduce-scatter.4
  146.7 60.5 all-gather.9
  209.3 91.7 all-gather.7
  303.9 21.2 reduce-scatter.6
  328.8 83.5 reduce-scatter.8
  415.2 45.1 all-gather.11
  463.1 59.9 all-gather.15
  525.4 32.8 all-gather.13
  560.6 38.4 reduce-scatter.10
